TPU v7x, 128 devices: a whole 4x4x4 slice. The times are simulated.
128 devices in a mesh: win: 4 (over z_lo, core), chan: 32 (over y, z_hi, x).
Axes of the slice: x: 4, y: 4, z: 4 (z_hi: 2, z_lo: 2; z = z_hi * 2 + z_lo), core: 2. Of those that a mesh axis runs over, the one named last changes fastest.
Arguments:
- traces: bfloat16 [32, 1024, 7680], P('win', 'chan'), may hold values from -6 to 6
- filter_taps: bfloat16 [32], replicated, may hold values from 0.019897461 to 0.14941406
- good_channels: int32 [1024], P('chan'), may hold values 0 or 1
- source_index: int32 [256], replicated, may hold values from 0 to 1023, as said below
Outputs:
- correlations: float32 [256, 1024, 2048], P('win', 'chan')
Inputs may be any that keep to these rules, and one draw needn't show every extreme that they name: `source_index`: 256 distinct channel numbers; channels 0 and 1023 are among them; how many fall in one device's block varies.
All inputs are finite; a program needn't handle non-finite values. No bound on the sum of `good_channels` on one device may be relied on, other than what follows from the above.
Results may differ from a plain program's by a relative error of at most 0.0071.
Values may be sent and summed in bfloat16 or wider, within the bound.
A program may use at most 192 MiB of HBM per device.

v0:
```python
import math
import jax
import jax.numpy as jnp
from jax import lax
from jax.sharding import PartitionSpec as P

L = 7680
F = 512
LAGS = 2048
HALO = 16
SMOOTH = 64
K0 = 31


def turn(bins, steps):
    phase = jnp.mod(bins * steps, L).astype(jnp.float32) * (2.0 * math.pi / L)
    return (jnp.cos(phase), jnp.sin(phase))


def forward_table():
    bins = K0 + jnp.arange(F, dtype=jnp.int32)
    step = 64
    ca, sa = turn(bins[None, :], step * jnp.arange(L // step, dtype=jnp.int32)[:, None])
    cb, sb = turn(bins[None, :], jnp.arange(step, dtype=jnp.int32)[:, None])
    ca, sa, cb, sb = lax.optimization_barrier((ca, sa, cb, sb))
    cosine = ca[:, None] * cb[None] - sa[:, None] * sb[None]
    sine = sa[:, None] * cb[None] + ca[:, None] * sb[None]
    return (cosine.reshape(L, F).astype(jnp.bfloat16), (-sine).reshape(L, F).astype(jnp.bfloat16))


def inverse_table():
    bins = (K0 + jnp.arange(F, dtype=jnp.int32))[:, None]
    step = 128
    ca, sa = turn(bins, step * jnp.arange(LAGS // step, dtype=jnp.int32)[None, :] - LAGS // 2)
    cb, sb = turn(bins, jnp.arange(step, dtype=jnp.int32)[None, :])
    ca, sa, cb, sb = lax.optimization_barrier((ca, sa, cb, sb))
    cosine = ca[:, :, None] * cb[:, None] - sa[:, :, None] * sb[:, None]
    sine = sa[:, :, None] * cb[:, None] + ca[:, :, None] * sb[:, None]
    return (
        cosine.reshape(F, LAGS).astype(jnp.bfloat16),
        (-sine).reshape(F, LAGS).astype(jnp.bfloat16),
    )


def smoothing():
    positions = jnp.arange(F, dtype=jnp.int32)
    near = (jnp.abs(positions[:, None] - positions[None, :]) <= SMOOTH).astype(jnp.float32)
    return near / jnp.sum(near, axis=0, keepdims=True)


def make_band(filter_taps, channel_count):
    kernel = jnp.concatenate(
        [
            -filter_taps[:HALO].astype(jnp.float32),
            jnp.ones((1,), jnp.float32),
            -filter_taps[HALO:].astype(jnp.float32),
        ]
    )
    row_ids = jnp.arange(channel_count, dtype=jnp.int32)[:, None]
    columns = jnp.arange(channel_count + 2 * HALO, dtype=jnp.int32)[None, :]
    offset = columns - row_ids
    choose = offset[:, :, None] == jnp.arange(2 * HALO + 1, dtype=jnp.int32)[None, None, :]
    return jnp.sum(jnp.where(choose, kernel[None, None, :], 0.0), axis=2)


def with_halo(cells, axis, dim, width):
    count = lax.axis_size(axis)
    ends = count - 1
    head = lax.slice_in_dim(cells, 0, width, axis=dim)
    tail = lax.slice_in_dim(cells, cells.shape[dim] - width, cells.shape[dim], axis=dim)
    before = lax.ppermute(tail, axis, [(i, (i + 1) % count) for i in range(ends)])
    after = lax.ppermute(head, axis, [((i + 1) % count, i) for i in range(ends)])
    return jnp.concatenate([before, cells, after], axis=dim)


def per_device(traces, filter_taps, good_channels, source_index):
    windows, channels, length = traces.shape
    groups, blocks = (lax.axis_size("win"), lax.axis_size("chan"))
    sources = source_index.shape[0]
    bins = F // blocks
    everyone = channels * blocks
    good = good_channels.astype(jnp.float32)[None, :, None]
    rows = traces.reshape(windows * channels, length)
    cosine, sine = forward_table()
    dot = lambda a, b: jnp.dot(a, b, preferred_element_type=jnp.float32)
    spectrum = jnp.stack([dot(rows, cosine), dot(rows, sine)], axis=1)
    spectrum = spectrum.reshape(windows, channels, 2 * F) * good
    padded = with_halo(spectrum, "chan", 1, HALO)
    band = make_band(filter_taps, channels)
    filtered = jnp.einsum("cd,wdf->wcf", band, padded, precision=lax.Precision.HIGHEST) * good
    real, imag = (filtered[..., :F], filtered[..., F:])
    magnitude = jnp.sqrt(real * real + imag * imag).reshape(-1, F)
    amplitude = jnp.dot(magnitude, smoothing(), precision=lax.Precision.HIGHEST)
    divisor = amplitude.reshape(real.shape) + 1e-06
    whitened = jnp.stack([real / divisor, imag / divisor], axis=2).astype(jnp.bfloat16)
    split = whitened.reshape(windows, channels, 2, blocks, bins)
    split = jnp.transpose(split, (3, 4, 2, 0, 1)).reshape(blocks, bins * 2, windows * channels)
    mixed = lax.all_to_all(split, "chan", 0, 0, tiled=True)
    mixed = mixed.reshape(blocks, bins * 2 * windows, channels)
    mixed = jnp.transpose(mixed, (1, 0, 2)).reshape(bins * 2 * windows, everyone)
    ids = jnp.arange(everyone, dtype=jnp.int32)
    selector = (ids[:, None] == source_index[None, :]).astype(jnp.bfloat16)
    picked = dot(mixed, selector).astype(jnp.bfloat16)
    share = sources // groups
    picked = picked.reshape(bins * 2 * windows, groups, share)
    picked = jnp.transpose(picked, (1, 0, 2))
    picked = lax.all_to_all(picked, "win", 0, 0, tiled=True)
    picked = picked.reshape(groups, bins, 2, windows, share)
    picked = jnp.transpose(picked, (1, 2, 0, 3, 4)).reshape(bins, groups * windows, 2 * share)
    gathered = lax.all_gather(picked, "chan", axis=0, tiled=True)
    gathered = gathered.reshape(F, 2 * groups * windows, share)
    own = lax.all_gather(whitened, "win", axis=0, tiled=True)
    own = jnp.transpose(own, (3, 2, 0, 1))
    own_real, own_imag = (own[:, 0], own[:, 1])
    left = jnp.concatenate([own_real, own_imag], axis=1)
    right = jnp.concatenate([own_imag, -own_real], axis=1)
    both = jnp.concatenate([left, right], axis=2)
    stacked = jnp.einsum("fks,fkc->fsc", gathered, both, preferred_element_type=jnp.float32)
    stacked = stacked.astype(jnp.bfloat16).reshape(F, share, 2, channels)
    stacked = jnp.transpose(stacked, (1, 3, 2, 0)).reshape(share * channels, 2, F)
    scaling = 1.0 / math.sqrt(F * windows * groups)
    cosine, sine = inverse_table()
    lagged = (dot(stacked[:, 0], cosine) + dot(stacked[:, 1], sine)) * scaling
    return lagged.reshape(share, channels, LAGS)


def solution(mesh):
    placed = (P("win", "chan", None), P(), P("chan"), P())
    return jax.shard_map(
        per_device, mesh=mesh, in_specs=placed, out_specs=P("win", "chan", None), check_vma=False
    )
```

profile of v0, /device:TPU:0, one launch (start us, length us, event | category | flops | bytes accessed | tf_op | source)
XLA Modules:
  0.0 244.9 jit_solution(9256046249764488601)
XLA Ops:
  6.5 0.5 fusion.53
  7.1 1.1 fusion.46
  8.2 4.6 %subtract_convert_fusion = (bf16[120,64,512]{2,1,0:T(8,128)(2,1)S(1)}, bf16[120,64,512]{2,1,0:T(8,128)(2,1)S(1)}) fusion(f32[64,512]{1,0:T(8,128)S(1)} %get-tuple-element.16, f32[120,512]{1,0:T(8,128)S(1)} %get-tuple-element.15, f32[64,512]{1,0:T(8,128)S(1)} %get-tuple-element.14, f32[120,512]{1,0:T(8,128)S(1)} %get-tuple-element.13), kind=kLoop, calls=%fused_computation.2 | loop fusion | flops 35389440 | bytes 16482304 | tf_op jit(solution)/shard_map/convert_element_type | solution.py:28
  12.8 2.2 convolution_bitcast_fusion
  15.1 2.2 convolution_bitcast_fusion.1
  17.4 0.6 copy.31
  18.0 0.9 reshape.176
  18.9 0.2 broadcast_multiply_fusion
  19.1 0.1 fusion.60
  19.2 3.5 %collective-permute-start = (f32[8,16,1024]{2,1,0:T(8,128)S(1)}, f32[8,16,1024]{2,1,0:T(8,128)S(1)}, u32[]{:S(2)}, u32[]{:S(2)}) collective-permute-start(f32[8,16,1024]{2,1,0:T(8,128)S(1)} %get-tuple-element.27), channel_id=1, source_target_pairs={{0,1},{1,2},{2,3},{3,4},{4,5},{5,6},{6,7},{7,8},{8,9},{9,10},{10,1... | collective-permute-start | bytes 1572872 | tf_op jit(solution)/shard_map/ppermute | solution.py:71
  22.8 1.3 collective-permute-start.1
  24.1 0.1 convert_reduce_fusion
  24.3 0.1 pad_maximum_fusion.2
  24.4 0.1 select_reduce_fusion
  24.5 9.4 %collective-permute-done = f32[8,16,1024]{2,1,0:T(8,128)S(1)} collective-permute-done((f32[8,16,1024]{2,1,0:T(8,128)S(1)}, f32[8,16,1024]{2,1,0:T(8,128)S(1)}, u32[]{:S(2)}, u32[]{:S(2)}) %collective-permute-start) | collective-permute-done | bytes 524320 | tf_op jit(solution)/shard_map/ppermute | solution.py:71
  33.9 4.1 %collective-permute-done.1 = f32[8,16,1024]{2,1,0:T(8,128)S(1)} collective-permute-done((f32[8,16,1024]{2,1,0:T(8,128)S(1)}, f32[8,16,1024]{2,1,0:T(8,128)S(1)}, u32[]{:S(2)}, u32[]{:S(2)}) %collective-permute-start.1) | collective-permute-done | bytes 524320 | tf_op jit(solution)/shard_map/ppermute | solution.py:72
  38.1 1.2 fusion.14
  39.3 1.3 divide_convert_fusion.1
  40.6 0.8 pad_maximum_fusion.1
  41.4 0.2 all-gather.3.cloned.1.call-start
  41.7 0.5 copy.32
  42.2 0.5 copy.33
  42.6 0.5 maximum_bitcast_fusion
  43.1 2.4 copy.34
  45.6 1.5 reshape.177
  47.0 25.4 %all_to_all.10 = bf16[32,32,256]{2,1,0:T(8,128)(2,1)S(1)} all-to-all(bf16[32,32,256]{2,1,0:T(8,128)(2,1)S(1)} %reshape.177), channel_id=1, replica_groups=mesh['win'=4,'chan'=32] {'chan'}, dimensions={0} | all-to-all | bytes 1048576 | tf_op jit(solution)/shard_map/all_to_all | solution.py:98
  72.5 0.9 reshape.178
  73.4 0.8 copy.35
  74.2 0.5 convolution_convert_fusion.1
  74.7 9.1 %all_to_all.11 = bf16[4,256,64]{1,2,0:T(8,128)(2,1)S(1)} all-to-all(bf16[4,256,64]{1,2,0:T(8,128)(2,1)S(1)} %bitcast.90), channel_id=1, replica_groups=mesh['win'=4,'chan'=32] {'win'}, dimensions={0} | all-to-all | bytes 262144 | tf_op jit(solution)/shard_map/all_to_all | solution.py:107
  83.8 0.2 copy.36
  84.0 0.8 reshape.182
  84.9 1.1 fusion.34
  86.0 1.1 fusion.38
  87.1 5.5 %negate_convert_fusion.1 = (bf16[512,16,128]{2,1,0:T(8,128)(2,1)S(1)}, bf16[512,16,128]{2,1,0:T(8,128)(2,1)}) fusion(f32[512,128]{1,0:T(8,128)S(1)} %get-tuple-element.20, f32[512,16]{1,0:T(8,128)S(1)} %get-tuple-element.19, f32[512,128]{1,0:T(8,128)S(1)} %get-tuple-element.18, f32[512,16]{1,0:T(8,128)S(1)} %get-tuple-element.17), kind=kLoop, calls=%fused_computation.5 | loop fusion | flops 9437184 | bytes 4784128 | tf_op jit(solution)/shard_map/convert_element_type | solution.py:41
  92.7 1.3 fusion.59
  94.0 1.8 slice_bitcast_fusion.5
  95.8 2.2 maximum_maximum_fusion
  98.0 13.0 %copy.40 = bf16[512,64,64]{2,1,0:T(8,128)(2,1)} copy(bf16[512,64,64]{0,2,1:T(8,128)(2,1)} %maximum_maximum_fusion) | data formatting | bytes 8388608 | tf_op jit(solution)/shard_map/concatenate | solution.py:117
  111.0 59.2 %all-gather.3.cloned.1.call-done = bf16[512,32,128]{2,1,0:T(8,128)(2,1)} async-done(((bf16[16,32,128]{2,1,0:T(8,128)(2,1)}), bf16[512,32,128]{2,1,0:T(8,128)(2,1)}) %all-gather.3.cloned.1.call-update) | async-done | bytes 4194320 | tf_op jit(solution)/shard_map/all_gather | solution.py:110
  170.2 7.6 %copy.38 = bf16[512,32,128]{0,2,1:T(8,128)(2,1)} copy(bf16[512,32,128]{2,1,0:T(8,128)(2,1)} %all-gather.3.cloned.1.call-done) | data formatting | bytes 8388608 | tf_op jit(solution)/shard_map/all_gather | solution.py:110
  177.8 15.6 %copy.39 = bf16[512,64,64]{1,2,0:T(8,128)(2,1)} copy(bf16[512,64,64]{0,2,1:T(8,128)(2,1)} %bitcast.73) | data formatting | bytes 8388608 | tf_op jit(solution)/shard_map/reshape | solution.py:111
  193.4 11.3 %convolution_convert_fusion = bf16[512,64,64]{2,1,0:T(8,128)(2,1)} fusion(bf16[512,64,64]{1,2,0:T(8,128)(2,1)} %copy.39, bf16[512,64,64]{2,1,0:T(8,128)(2,1)} %copy.40), kind=kOutput, calls=%fused_computation.3 | convolution fusion | flops 270532608 | bytes 12582912 | tf_op jit(solution)/shard_map/fks,fkc->fsc/dot_general | solution.py:118
  204.7 9.7 %copy.41 = bf16[512,64,64]{0,2,1:T(8,128)(2,1)} copy(bf16[512,64,64]{2,1,0:T(8,128)(2,1)} %convolution_convert_fusion) | data formatting | bytes 8388608 | tf_op jit(solution)/shard_map/convert_element_type | solution.py:119
  214.4 2.7 %copy.42 = bf16[64,32,2,512]{3,1,0,2:T(8,128)(2,1)S(1)} copy(bf16[64,32,2,512]{3,1,2,0:T(8,128)(2,1)} %bitcast.74) | data formatting | bytes 8388608 | tf_op jit(solution)/shard_map/transpose | solution.py:120
  217.1 0.2 copy-done
  217.3 8.7 %fusion.2 = f32[2048,2048]{1,0:T(8,128)} fusion(bf16[64,8,16,128]{3,2,1,0:T(8,128)(2,1)S(1)} %bitcast.85, bf16[2048,2,512]{2,0,1:T(8,128)(2,1)S(1)} %bitcast.75), kind=kOutput, calls=%fused_computation.9 | convolution fusion | flops 4294967296 | bytes 20971520 | tf_op jit(solution)/shard_map/dot_general | solution.py:85
  226.0 12.0 %add_multiply_fusion = f32[2048,2048]{1,0:T(8,128)} fusion(f32[2048,2048]{1,0:T(8,128)} %fusion.2, bf16[64,8,16,128]{3,2,1,0:T(8,128)(2,1)S(1)} %bitcast.77, bf16[2048,2,512]{2,0,1:T(8,128)(2,1)S(1)} %bitcast.76), kind=kOutput, calls=%fused_computation | convolution fusion | flops 4303355904 | bytes 37748736 | tf_op jit(solution)/shard_map/dot_general | solution.py:85
  (21 shorter events, 0.3 us)
Async XLA Ops:
  6.5 86.1 %all-gather.5.cloned.1.call-start = ((), (), s32[]{:S(2)}) async-start(), calls=%async_computation.3 | async-start | bytes 2621440 | tf_op jit(solution)/shard_map/all_gather | solution.py:112
  8.2 4.7 %copy-start.2 = (bf16[8,32,7680]{2,1,0:T(8,128)(2,1)S(1)}, bf16[8,32,7680]{2,1,0:T(8,128)(2,1)}, u32[]{:S(2)}) copy-start(bf16[8,32,7680]{2,1,0:T(8,128)(2,1)} %param.4) | copy-start | bytes 11796484
  17.3 1.6 copy-start.4
  17.4 6.8 %copy-start.1 = (bf16[32]{0:T(256)(128)(2,1)S(1)}, bf16[32]{0:T(256)(128)(2,1)}, u32[]{:S(2)}) copy-start(bf16[32]{0:T(256)(128)(2,1)} %param.5) | copy-start | bytes 196
  19.2 14.7 %collective-permute-start = (f32[8,16,1024]{2,1,0:T(8,128)S(1)}, f32[8,16,1024]{2,1,0:T(8,128)S(1)}, u32[]{:S(2)}, u32[]{:S(2)}) collective-permute-start(f32[8,16,1024]{2,1,0:T(8,128)S(1)} %get-tuple-element.27), channel_id=1, source_target_pairs={{0,1},{1,2},{2,3},{3,4},{4,5},{5,6},{6,7},{7,8},{8,9},{9,10},{10,1... | collective-permute-start | bytes 1572872 | tf_op jit(solution)/shard_map/ppermute | solution.py:71
  22.8 15.3 %collective-permute-start.1 = (f32[8,16,1024]{2,1,0:T(8,128)S(1)}, f32[8,16,1024]{2,1,0:T(8,128)S(1)}, u32[]{:S(2)}, u32[]{:S(2)}) collective-permute-start(f32[8,16,1024]{2,1,0:T(8,128)S(1)} %get-tuple-element.28), channel_id=1, source_target_pairs={{1,0},{2,1},{3,2},{4,3},{5,4},{6,5},{7,6},{8,7},{9,8},{10,9},{11,1... | collective-permute-start | bytes 1572872 | tf_op jit(solution)/shard_map/ppermute | solution.py:72
  41.4 128.8 %all-gather.3.cloned.1.call-start = ((), (), s32[]{:S(2)}) async-start(), calls=%async_computation.2 | async-start | bytes 4325376 | tf_op jit(solution)/shard_map/all_gather | solution.py:110
  45.6 28.6 %copy-start.3 = (s32[256]{0:T(256)S(1)}, s32[256]{0:T(256)}, u32[]{:S(2)}) copy-start(s32[256]{0:T(256)} %param.7) | copy-start | bytes 3076
  214.4 2.9 %copy-start = (bf16[512,16,128]{2,1,0:T(8,128)(2,1)S(1)}, bf16[512,16,128]{2,1,0:T(8,128)(2,1)}, u32[]{:S(2)}) copy-start(bf16[512,16,128]{2,1,0:T(8,128)(2,1)} %get-tuple-element.26) | copy-start | bytes 6291460
Sparse Core Ops, SparseCore 0:
  41.6 41.6 all-gather.4
  86.2 83.9 all-gather.2
where the time goes:
time: 246 us; the launch traced here: 245 us
  waiting for transfers between devices  72.8 us (30%)
  local copies, waits for them, and re-layouts  59.7 us (24%)
  matrix products  39.6 us (16%)
  blocking collectives  34.5 us (14%)
  other arithmetic  19.5 us (8%)
  between operations  13.7 us (6%)
  starting transfers between devices  5.06 us (2%)
    all_gather x1, waiting for transfers between devices, per_device(): gathered = lax.all_gather(picked, 'chan', axis=0, tiled=True)  59.2 us
    dot_general x5, matrix products, per_device(): dot = lambda a, b: jnp.dot(a, b, preferred_element_type=jnp.float32)  25.7 us
    all_to_all x1, blocking collectives, per_device(): mixed = lax.all_to_all(split, 'chan', 0, 0, tiled=True)  25.4 us
    reshape x1, local copies, waits for them, and re-layouts, per_device(): gathered = gathered.reshape(F, 2 * groups * windows, share)  15.6 us
    concatenate x1, local copies, waits for them, and re-layouts, per_device(): both = jnp.concatenate([left, right], axis=2)  13 us
    dot_general x1, matrix products, per_device(): jnp.einsum('fks,fkc->fsc', gathered, both, preferred_element_type=jnp.flo...  11.3 us
    convert_element_type x1, local copies, waits for them, and re-layouts, per_device(): stacked = stacked.astype(jnp.bfloat16).reshape(F, share, 2, channels)  9.74 us
    ppermute x1, waiting for transfers between devices, with_halo(): lax.ppermute(tail, axis, [(i, (i + 1) % count) for i in range(ends)])  9.4 us
  transfers between devices with their start and end apart: 4, of which 3 were waited for; matrix products, arithmetic and copies ran while one was open for 14% of the time, Pallas kernels for 0%

commit v1 on v0

--- a/solution.py
+++ b/solution.py
@@ -107,7 +107,9 @@
     picked = lax.all_to_all(picked, "win", 0, 0, tiled=True)
     picked = picked.reshape(groups, bins, 2, windows, share)
     picked = jnp.transpose(picked, (1, 2, 0, 3, 4)).reshape(bins, groups * windows, 2 * share)
-    gathered = lax.all_gather(picked, "chan", axis=0, tiled=True)
+    gathered = jnp.concatenate(
+        lax.all_to_all(jnp.stack([picked] * lax.axis_size("chan")), "chan", 0, 0), axis=0
+    )
     gathered = gathered.reshape(F, 2 * groups * windows, share)
     own = lax.all_gather(whitened, "win", axis=0, tiled=True)
     own = jnp.transpose(own, (3, 2, 0, 1))

time: 246 us -> 232 us (0.943)
  local copies, waits for them, and re-layouts: 59.7 us -> 49.9 us
  blocking collectives: 34.5 us -> 25.4 us
  starting transfers between devices: 5.06 us -> 13.5 us
  waiting for transfers between devices: 72.8 us -> 69.5 us
    all_gather x1 -> x0, waiting for transfers between devices: 59.2 us -> none  [per_device(): gathered = lax.all_gather(picked, 'chan', axis=0, tiled=True)]
    all_gather x1, waiting for transfers between devices: 0.01 us -> 52.5 us  [per_device(): own = lax.all_gather(whitened, 'win', axis=0, tiled=True)]
    reshape x2 -> x0, local copies, waits for them, and re-layouts: 16.4 us -> none  [the longest x1 15.6 us: per_device(): gathered = gathered.reshape(F, 2 * groups * windows, share)]
    another operation x2 -> x5, local copies, waits for them, and re-layouts: 0.96 us -> 15.1 us  [the longest x1 11 us: per_device(): gathered = gathered.reshape(F, 2 * groups * windows, share)]
    all_to_all x1 -> x0, blocking collectives: 9.1 us -> none  [per_device(): picked = lax.all_to_all(picked, 'win', 0, 0, tiled=True)]
    all_to_all x0 -> x2, starting transfers between devices: none -> 8.42 us  [the longest x1 5.1 us: per_device(): lax.all_to_all(jnp.stack([picked] * lax.axis_size('chan')), 'chan', 0, 0)]
    all_gather x1 -> x0, local copies, waits for them, and re-layouts: 7.55 us -> none  [per_device(): gathered = lax.all_gather(picked, 'chan', axis=0, tiled=True)]
    all_to_all x0 -> x2, waiting for transfers between devices: none -> 3.64 us  [the longest x1 3.64 us: per_device(): picked = lax.all_to_all(picked, 'win', 0, 0, tiled=True)]
  transfers between devices with their start and end apart: 4 -> 5, of which waited for: 3 -> 4; matrix products, arithmetic and copies ran while one was open for 14% -> 13% of each run, Pallas kernels for 0% -> 0%
where the time goes in v1:
time: 232 us; the launch traced here: 230 us
  waiting for transfers between devices  69.5 us (30%)
  local copies, waits for them, and re-layouts  49.9 us (22%)
  matrix products  38.1 us (16%)
  blocking collectives  25.4 us (11%)
  other arithmetic  19.5 us (8%)
  between operations  13.7 us (6%)
  starting transfers between devices  13.5 us (6%)
    all_gather x1, waiting for transfers between devices, per_device(): own = lax.all_gather(whitened, 'win', axis=0, tiled=True)  52.5 us
    dot_general x5, matrix products, per_device(): dot = lambda a, b: jnp.dot(a, b, preferred_element_type=jnp.float32)  26.3 us
    all_to_all x1, blocking collectives, per_device(): mixed = lax.all_to_all(split, 'chan', 0, 0, tiled=True)  25.4 us
    concatenate x1, local copies, waits for them, and re-layouts, per_device(): both = jnp.concatenate([left, right], axis=2)  13 us
    another operation x1, local copies, waits for them, and re-layouts, per_device(): gathered = gathered.reshape(F, 2 * groups * windows, share)  11 us
    convert_element_type x1, local copies, waits for them, and re-layouts, per_device(): stacked = stacked.astype(jnp.bfloat16).reshape(F, share, 2, channels)  9.74 us
    dot_general x1, matrix products, per_device(): jnp.einsum('fks,fkc->fsc', gathered, both, preferred_element_type=jnp.flo...  9.32 us
    ppermute x1, waiting for transfers between devices, with_halo(): lax.ppermute(tail, axis, [(i, (i + 1) % count) for i in range(ends)])  9.22 us
  transfers between devices with their start and end apart: 5, of which 4 were waited for; matrix products, arithmetic and copies ran while one was open for 13% of the time, Pallas kernels for 0%

profile of v1, /device:TPU:0, one launch (start us, length us, event | category | flops | bytes accessed | tf_op | source)
XLA Modules:
  0.0 229.7 jit_solution(9359476464815870908)
XLA Ops:
  6.5 0.5 fusion.53
  7.1 1.1 fusion.46
  8.2 4.6 %subtract_convert_fusion = (bf16[120,64,512]{2,1,0:T(8,128)(2,1)S(1)}, bf16[120,64,512]{2,1,0:T(8,128)(2,1)S(1)}) fusion(f32[64,512]{1,0:T(8,128)S(1)} %get-tuple-element.16, f32[120,512]{1,0:T(8,128)S(1)} %get-tuple-element.15, f32[64,512]{1,0:T(8,128)S(1)} %get-tuple-element.14, f32[120,512]{1,0:T(8,128)S(1)} %get-tuple-element.13), kind=kLoop, calls=%fused_computation.2 | loop fusion | flops 35389440 | bytes 16482304 | tf_op jit(solution)/shard_map/convert_element_type | solution.py:28
  12.8 2.2 convolution_bitcast_fusion
  15.1 2.2 convolution_bitcast_fusion.1
  17.4 0.6 copy.29
  18.0 0.9 reshape.172
  18.9 0.2 broadcast_multiply_fusion
  19.1 0.1 fusion.60
  19.2 3.5 %collective-permute-start = (f32[8,16,1024]{2,1,0:T(8,128)S(1)}, f32[8,16,1024]{2,1,0:T(8,128)S(1)}, u32[]{:S(2)}, u32[]{:S(2)}) collective-permute-start(f32[8,16,1024]{2,1,0:T(8,128)S(1)} %get-tuple-element.27), channel_id=1, source_target_pairs={{0,1},{1,2},{2,3},{3,4},{4,5},{5,6},{6,7},{7,8},{8,9},{9,10},{10,1... | collective-permute-start | bytes 1572872 | tf_op jit(solution)/shard_map/ppermute | solution.py:71
  22.8 1.5 collective-permute-start.1
  24.3 0.1 convert_reduce_fusion
  24.5 0.1 select_reduce_fusion
  24.7 9.2 %collective-permute-done = f32[8,16,1024]{2,1,0:T(8,128)S(1)} collective-permute-done((f32[8,16,1024]{2,1,0:T(8,128)S(1)}, f32[8,16,1024]{2,1,0:T(8,128)S(1)}, u32[]{:S(2)}, u32[]{:S(2)}) %collective-permute-start) | collective-permute-done | bytes 524320 | tf_op jit(solution)/shard_map/ppermute | solution.py:71
  33.9 4.1 %collective-permute-done.1 = f32[8,16,1024]{2,1,0:T(8,128)S(1)} collective-permute-done((f32[8,16,1024]{2,1,0:T(8,128)S(1)}, f32[8,16,1024]{2,1,0:T(8,128)S(1)}, u32[]{:S(2)}, u32[]{:S(2)}) %collective-permute-start.1) | collective-permute-done | bytes 524320 | tf_op jit(solution)/shard_map/ppermute | solution.py:72
  38.1 1.2 fusion.14
  39.3 1.3 divide_convert_fusion.1
  40.6 0.5 copy.30
  41.1 0.5 copy.31
  41.6 0.5 maximum_bitcast_fusion
  42.1 2.4 %copy.32 = bf16[32,16,2,8,32]{4,3,2,1,0:T(8,128)(2,1)S(1)} copy(bf16[32,16,2,8,32]{4,1,0,3,2:T(8,128)(2,1)S(1)} %maximum_bitcast_fusion) | data formatting | bytes 1048576 | tf_op jit(solution)/shard_map/transpose | solution.py:97
  44.5 1.5 reshape.173
  46.0 25.4 %all_to_all.15 = bf16[32,32,256]{2,1,0:T(8,128)(2,1)S(1)} all-to-all(bf16[32,32,256]{2,1,0:T(8,128)(2,1)S(1)} %reshape.173), channel_id=1, replica_groups=mesh['win'=4,'chan'=32] {'chan'}, dimensions={0} | all-to-all | bytes 1048576 | tf_op jit(solution)/shard_map/all_to_all | solution.py:98
  71.4 0.9 reshape.174
  72.3 0.8 copy.33
  73.1 1.2 convolution_convert_fusion.1
  74.3 3.3 %all-to-all-start.1 = ((bf16[4,256,64]{1,2,0:T(8,128)(2,1)}), bf16[4,256,64]{1,2,0:T(8,128)(2,1)S(1)}, u32[]{:S(2)}, u32[]{:S(2)}) async-start(bf16[4,256,64]{1,2,0:T(8,128)(2,1)} %bitcast.16), calls=%async_computation.1 | async-start | bytes 262144 | tf_op jit(solution)/shard_map/all_to_all | solution.py:107
  77.7 0.8 pad_maximum_fusion.1
  78.5 3.6 %all-to-all-done.1 = bf16[4,256,64]{1,2,0:T(8,128)(2,1)S(1)} async-done(((bf16[4,256,64]{1,2,0:T(8,128)(2,1)}), bf16[4,256,64]{1,2,0:T(8,128)(2,1)S(1)}, u32[]{:S(2)}, u32[]{:S(2)}) %all-to-all-start.1) | async-done | bytes 131104 | tf_op jit(solution)/shard_map/all_to_all | solution.py:107
  82.2 0.2 copy.34
  82.4 0.1 stack_reshape.2
  82.6 3.0 %stack.36 = bf16[32,16,32,128]{3,2,1,0:T(8,128)(2,1)} broadcast(bf16[16,32,128]{2,1,0:T(8,128)(2,1)S(1)} %stack_reshape.2), dimensions={1,2,3} | broadcast | bytes 4325376 | tf_op jit(solution)/shard_map/stack | solution.py:111
  85.5 5.1 %all-to-all-start.2 = ((bf16[32,16,32,128]{3,2,1,0:T(8,128)(2,1)}), bf16[32,16,32,128]{3,2,1,0:T(8,128)(2,1)}, u32[]{:S(2)}, u32[]{:S(2)}) async-start(bf16[32,16,32,128]{3,2,1,0:T(8,128)(2,1)} %stack.36), calls=%async_computation.2 | async-start | bytes 8388608 | tf_op jit(solution)/shard_map/all_to_all | solution.py:111
  90.6 1.1 fusion.34
  91.8 1.1 fusion.38
  92.9 5.5 %negate_convert_fusion.1 = (bf16[512,16,128]{2,1,0:T(8,128)(2,1)S(1)}, bf16[512,16,128]{2,1,0:T(8,128)(2,1)}) fusion(f32[512,128]{1,0:T(8,128)S(1)} %get-tuple-element.20, f32[512,16]{1,0:T(8,128)S(1)} %get-tuple-element.19, f32[512,128]{1,0:T(8,128)S(1)} %get-tuple-element.18, f32[512,16]{1,0:T(8,128)S(1)} %get-tuple-element.17), kind=kLoop, calls=%fused_computation.5 | loop fusion | flops 9437184 | bytes 4784128 | tf_op jit(solution)/shard_map/convert_element_type | solution.py:41
  98.4 52.5 %all-gather.2.cloned.1.call-done = bf16[32,32,2,512]{3,1,0,2:T(8,128)(2,1)} async-done(((bf16[8,32,2,512]{3,1,0,2:T(8,128)(2,1)}), bf16[32,32,2,512]{3,1,0,2:T(8,128)(2,1)}) %all-gather.2.cloned.1.call-update) | async-done | bytes 2097168 | tf_op jit(solution)/shard_map/all_gather | solution.py:114
  151.0 1.3 fusion.59
  152.2 1.8 slice_bitcast_fusion.5
  154.0 2.2 maximum_maximum_fusion
  156.2 13.0 %copy.37 = bf16[512,64,64]{2,1,0:T(8,128)(2,1)} copy(bf16[512,64,64]{0,2,1:T(8,128)(2,1)} %maximum_maximum_fusion) | data formatting | bytes 8388608 | tf_op jit(solution)/shard_map/concatenate | solution.py:119
  169.2 11.0 %reshape_reshape.3 = bf16[512,64,64]{2,1,0:T(8,128)(2,1)} reshape(bf16[32,16,32,128]{3,2,1,0:T(8,128)(2,1)} %all-to-all-done.2) | data formatting | bytes 8388608 | tf_op jit(solution)/shard_map/reshape;reshape | solution.py:113
  180.3 9.3 %convolution_convert_fusion = bf16[512,64,64]{2,1,0:T(8,128)(2,1)} fusion(bf16[512,64,64]{2,1,0:T(8,128)(2,1)} %reshape_reshape.3, bf16[512,64,64]{2,1,0:T(8,128)(2,1)} %copy.37), kind=kOutput, calls=%fused_computation.3 | convolution fusion | flops 270532608 | bytes 12582912 | tf_op jit(solution)/shard_map/fks,fkc->fsc/dot_general | solution.py:120
  189.6 9.7 %copy.38 = bf16[512,64,64]{0,2,1:T(8,128)(2,1)} copy(bf16[512,64,64]{2,1,0:T(8,128)(2,1)} %convolution_convert_fusion) | data formatting | bytes 8388608 | tf_op jit(solution)/shard_map/convert_element_type | solution.py:121
  199.3 2.7 %copy.39 = bf16[64,32,2,512]{3,1,0,2:T(8,128)(2,1)S(1)} copy(bf16[64,32,2,512]{3,1,2,0:T(8,128)(2,1)} %bitcast.74) | data formatting | bytes 8388608 | tf_op jit(solution)/shard_map/transpose | solution.py:122
  202.0 0.2 copy-done
  202.2 8.6 %fusion.2 = f32[2048,2048]{1,0:T(8,128)} fusion(bf16[64,8,16,128]{3,2,1,0:T(8,128)(2,1)S(1)} %bitcast.85, bf16[2048,2,512]{2,0,1:T(8,128)(2,1)S(1)} %bitcast.75), kind=kOutput, calls=%fused_computation.9 | convolution fusion | flops 4294967296 | bytes 20971520 | tf_op jit(solution)/shard_map/dot_general | solution.py:85
  210.8 12.0 %add_multiply_fusion = f32[2048,2048]{1,0:T(8,128)} fusion(f32[2048,2048]{1,0:T(8,128)} %fusion.2, bf16[64,8,16,128]{3,2,1,0:T(8,128)(2,1)S(1)} %bitcast.77, bf16[2048,2,512]{2,0,1:T(8,128)(2,1)S(1)} %bitcast.76), kind=kOutput, calls=%fused_computation | convolution fusion | flops 4303355904 | bytes 37748736 | tf_op jit(solution)/shard_map/dot_general | solution.py:85
  (25 shorter events, 0.4 us)
Async XLA Ops:
  8.2 4.7 %copy-start.4 = (bf16[8,32,7680]{2,1,0:T(8,128)(2,1)S(1)}, bf16[8,32,7680]{2,1,0:T(8,128)(2,1)}, u32[]{:S(2)}) copy-start(bf16[8,32,7680]{2,1,0:T(8,128)(2,1)} %param.4) | copy-start | bytes 11796484
  17.3 1.6 copy-start.6
  17.4 7.0 %copy-start.3 = (bf16[32]{0:T(256)(128)(2,1)S(1)}, bf16[32]{0:T(256)(128)(2,1)}, u32[]{:S(2)}) copy-start(bf16[32]{0:T(256)(128)(2,1)} %param.5) | copy-start | bytes 196
  19.2 14.7 %collective-permute-start = (f32[8,16,1024]{2,1,0:T(8,128)S(1)}, f32[8,16,1024]{2,1,0:T(8,128)S(1)}, u32[]{:S(2)}, u32[]{:S(2)}) collective-permute-start(f32[8,16,1024]{2,1,0:T(8,128)S(1)} %get-tuple-element.27), channel_id=1, source_target_pairs={{0,1},{1,2},{2,3},{3,4},{4,5},{5,6},{6,7},{7,8},{8,9},{9,10},{10,1... | collective-permute-start | bytes 1572872 | tf_op jit(solution)/shard_map/ppermute | solution.py:71
  22.8 15.3 %collective-permute-start.1 = (f32[8,16,1024]{2,1,0:T(8,128)S(1)}, f32[8,16,1024]{2,1,0:T(8,128)S(1)}, u32[]{:S(2)}, u32[]{:S(2)}) collective-permute-start(f32[8,16,1024]{2,1,0:T(8,128)S(1)} %get-tuple-element.28), channel_id=1, source_target_pairs={{1,0},{2,1},{3,2},{4,3},{5,4},{6,5},{7,6},{8,7},{9,8},{10,9},{11,1... | collective-permute-start | bytes 1572872 | tf_op jit(solution)/shard_map/ppermute | solution.py:72
  40.6 1.5 copy-start.1
  44.5 28.6 %copy-start.5 = (s32[256]{0:T(256)S(1)}, s32[256]{0:T(256)}, u32[]{:S(2)}) copy-start(s32[256]{0:T(256)} %param.7) | copy-start | bytes 3076
  71.4 6.3 %copy-start.2 = (bf16[8,32,512]{2,1,0:T(8,128)(2,1)S(1)}, bf16[8,32,512]{2,1,0:T(8,128)(2,1)}, u32[]{:S(2)}) copy-start(bf16[8,32,512]{2,1,0:T(8,128)(2,1)} %copy-done.1) | copy-start | bytes 786436
  74.3 7.9 %all-to-all-start.1 = ((bf16[4,256,64]{1,2,0:T(8,128)(2,1)}), bf16[4,256,64]{1,2,0:T(8,128)(2,1)S(1)}, u32[]{:S(2)}, u32[]{:S(2)}) async-start(bf16[4,256,64]{1,2,0:T(8,128)(2,1)} %bitcast.16), calls=%async_computation.1 | async-start | bytes 262144 | tf_op jit(solution)/shard_map/all_to_all | solution.py:107
  77.6 73.3 %all-gather.2.cloned.1.call-start = ((), (), s32[]{:S(2)}) async-start(), calls=%async_computation.3 | async-start | bytes 2621440 | tf_op jit(solution)/shard_map/all_gather | solution.py:114
  85.5 83.7 %all-to-all-start.2 = ((bf16[32,16,32,128]{3,2,1,0:T(8,128)(2,1)}), bf16[32,16,32,128]{3,2,1,0:T(8,128)(2,1)}, u32[]{:S(2)}, u32[]{:S(2)}) async-start(bf16[32,16,32,128]{3,2,1,0:T(8,128)(2,1)} %stack.36), calls=%async_computation.2 | async-start | bytes 8388608 | tf_op jit(solution)/shard_map/all_to_all | solution.py:111
  199.3 2.9 %copy-start = (bf16[512,16,128]{2,1,0:T(8,128)(2,1)S(1)}, bf16[512,16,128]{2,1,0:T(8,128)(2,1)}, u32[]{:S(2)}) copy-start(bf16[512,16,128]{2,1,0:T(8,128)(2,1)} %get-tuple-element.26) | copy-start | bytes 6291460
Sparse Core Ops, SparseCore 0:
  80.1 70.8 all-gather.1
